TPU v7x, 32 devices: a whole 2x2x4 slice. The times are simulated.
32 devices in a mesh: dp: 8 (over z, x), head: 4 (over y, core).
Axes of the slice: x: 2, y: 2, z: 4, core: 2. Of those that a mesh axis runs over, the one named last changes fastest.
Arguments:
- tokens: bfloat16 [32, 196, 216], P('dp'), may hold values from -6 to 6
- cotangent: float32 [32, 196, 216], P('dp'), may hold values from -6 to 6
- image_count: int32 [8], P('dp'), may hold values from 1 to 4, as said below
- subnet_heads: int32 [1], replicated, may hold values from 6 to 12
- subnet_width: int32 [1], replicated, may hold values from 432 to 864
- block_slot: int32 [12], replicated, may hold values from 0 to 15, as said below
- master: float32 [16, 54, 864], P('dp', None, 'head'), may hold values from -0.8164966 to 0.8164966
- master_m1: float32 [16, 54, 864], P('dp', None, 'head'), may hold values from -187.82971 to 187.82971
- master_m2: float32 [16, 54, 864], P('dp', None, 'head'), may hold values from 78 to 15680
- norm_params: float32 [4, 216], replicated, may hold values from -0.9 to 1.45
- norm_m1: float32 [4, 216], replicated, may hold values from -265.63132 to 265.63132
- norm_m2: float32 [4, 216], replicated, may hold values from 3920 to 35280
- talk: float32 [2, 12, 12], replicated, may hold values from -0.45 to 1.45
- talk_m1: float32 [2, 12, 12], replicated, may hold values from -831.55756 to 831.55756
- talk_m2: float32 [2, 12, 12], replicated, may hold values from 38416 to 307328
- conv: float32 [9, 864], P(None, 'head'), may hold values from -1 to 1
- conv_m1: float32 [9, 864], P(None, 'head'), may hold values from -108.41586 to 108.41586
- conv_m2: float32 [9, 864], P(None, 'head'), may hold values from 653 to 5226
Outputs:
- output: float32 [32, 196, 216], P('dp')
- token_grad: float32 [32, 196, 216], P('dp')
- new_master: float32 [16, 54, 864], P('dp', None, 'head')
- new_master_m1: float32 [16, 54, 864], P('dp', None, 'head')
- new_master_m2: float32 [16, 54, 864], P('dp', None, 'head')
- master_copy: bfloat16 [16, 54, 864], P('dp', None, 'head')
- new_norm: float32 [4, 216], replicated
- new_norm_m1: float32 [4, 216], replicated
- new_norm_m2: float32 [4, 216], replicated
- new_talk: float32 [2, 12, 12], replicated
- new_talk_m1: float32 [2, 12, 12], replicated
- new_talk_m2: float32 [2, 12, 12], replicated
- new_conv: float32 [9, 864], P(None, 'head')
- new_conv_m1: float32 [9, 864], P(None, 'head')
- new_conv_m2: float32 [9, 864], P(None, 'head')
Inputs may be any that keep to these rules, and one draw needn't show every extreme that they name: `image_count`: image slots at or beyond a dp index's count are padding; some dp index holds exactly 4 images and some exactly 1. `block_slot`: the twelve slots are distinct.
All inputs are finite; a program needn't handle non-finite values.
Results may differ from a plain program's by a relative error of at most 0.012.
The roundings to bfloat16 on the way count: a program that leaves them out, or rounds other values in their place, can miss the bound.
Values may be sent and summed in bfloat16 or wider, within the bound.
No kernel may reach another device: no remote copies, remote signals or barrier semaphores. Data moves between devices by JAX's collectives and lax.ppermute only.
A program may use at most 64 MiB of HBM per device.

v0:
```python
import jax
import jax.numpy as jnp
from jax import lax
from jax.sharding import PartitionSpec as P

HD = 18
SIDE = 14
norm_eps = 1e-05
beta_first = 0.5
beta_second = 0.5
adam_eps = 1e-08
rate_matrix = 0.06
rate_small = 0.2
decay_matrix = 0.05
adam_steps = 3
highest = lax.Precision.HIGHEST


def normalize(values, gain_row, bias_row):
    centred = values - jnp.mean(values, axis=-1, keepdims=True)
    inverse = lax.rsqrt(jnp.mean(centred * centred, axis=-1, keepdims=True) + norm_eps)
    scaled = centred * inverse
    return (scaled, inverse, scaled * gain_row + bias_row)


def normalize_back(grad_normed, scaled, inverse, gain_row):
    grad_scaled = grad_normed * gain_row
    centred_grad = grad_scaled - jnp.mean(grad_scaled, axis=-1, keepdims=True)
    return inverse * (
        centred_grad - scaled * jnp.mean(grad_scaled * scaled, axis=-1, keepdims=True)
    )


def pad_grid(values):
    images, length, channels = values.shape
    return jnp.pad(values.reshape(images, SIDE, SIDE, channels), ((0, 0), (1, 1), (1, 1), (0, 0)))


def shifted(padded, row_off, col_off):
    return padded[:, 1 + row_off : 1 + row_off + SIDE, 1 + col_off : 1 + col_off + SIDE, :]


def conv_grid(hidden, kernel):
    padded = pad_grid(hidden)
    summed = jnp.zeros_like(shifted(padded, 0, 0))
    for tap_index in range(9):
        summed = summed + kernel[tap_index] * shifted(padded, tap_index // 3 - 1, tap_index % 3 - 1)
    return summed.reshape(hidden.shape)


def conv_back(grad_act, hidden, kernel):
    padded_grad = pad_grid(grad_act)
    padded_hidden = pad_grid(hidden)
    grad_grid = shifted(padded_grad, 0, 0)
    grad_hidden = jnp.zeros_like(grad_grid)
    kernel_rows = []
    for tap_index in range(9):
        row_off = tap_index // 3 - 1
        col_off = tap_index % 3 - 1
        grad_hidden = grad_hidden + kernel[tap_index] * shifted(padded_grad, -row_off, -col_off)
        kernel_rows.append(
            jnp.sum(grad_grid * shifted(padded_hidden, row_off, col_off), axis=(0, 1, 2))
        )
    return (grad_hidden.reshape(hidden.shape), jnp.stack(kernel_rows))


def mix_scores(received, talk):
    pre_mixed = jnp.einsum(
        "mn,gnqk->gmqk", talk[0], received.astype(jnp.float32), precision=highest
    )
    softmaxed = jax.nn.softmax(pre_mixed, axis=-1)
    post_mixed = jnp.einsum("jm,gmqk->gjqk", talk[1], softmaxed, precision=highest).astype(
        jnp.bfloat16
    )
    return (softmaxed, post_mixed)


def mix_back(grad_post_all, softmaxed, received, talk):
    grad_soft = jnp.einsum("jm,gjqk->gmqk", talk[1], grad_post_all, precision=highest)
    talk_post = jnp.einsum("gjqk,gmqk->jm", grad_post_all, softmaxed, precision=highest)
    grad_mixed = softmaxed * (grad_soft - jnp.sum(grad_soft * softmaxed, axis=-1, keepdims=True))
    talk_pre = jnp.einsum(
        "gmqk,gnqk->mn", grad_mixed, received.astype(jnp.float32), precision=highest
    )
    grad_scores = jnp.einsum("mn,gmqk->gnqk", talk[0], grad_mixed, precision=highest).astype(
        jnp.bfloat16
    )
    return (grad_scores, talk_pre, talk_post)


def adamw(weights_old, gradient, moment_one, moment_two, step_rate, decay_rate):
    one_new = beta_first * moment_one + (1.0 - beta_first) * gradient
    two_new = beta_second * moment_two + (1.0 - beta_second) * gradient * gradient
    hat_one = one_new / (1.0 - beta_first**adam_steps)
    hat_two = two_new / (1.0 - beta_second**adam_steps)
    weights_new = weights_old - step_rate * (
        hat_one / (jnp.sqrt(hat_two) + adam_eps) + decay_rate * weights_old
    )
    return (weights_new, one_new, two_new)


def gather_blocks(master, block_slot):
    mine = master.astype(jnp.bfloat16)
    data_devices = lax.axis_size("dp")
    every = lax.all_to_all(
        jnp.broadcast_to(mine[None], (data_devices,) + mine.shape),
        "dp",
        split_axis=0,
        concat_axis=0,
        tiled=True,
    )
    every = every.reshape((data_devices * mine.shape[0],) + mine.shape[1:])
    return jnp.take(every, block_slot, axis=0)


def split_pair(values):
    high = lax.reduce_precision(values, exponent_bits=8, mantissa_bits=7)
    low = values - high
    return jnp.concatenate([high.astype(jnp.bfloat16), low.astype(jnp.bfloat16)], axis=-2)


def join_pair(values):
    rows = values.shape[-2] // 2
    return values[..., :rows, :].astype(jnp.float32) + values[..., rows:, :].astype(jnp.float32)


def local(
    tokens,
    cotangent,
    image_count,
    subnet_heads,
    subnet_width,
    block_slot,
    master,
    master_m1,
    master_m2,
    norm_params,
    norm_m1,
    norm_m2,
    talk,
    talk_m1,
    talk_m2,
    conv,
    conv_m1,
    conv_m2,
):
    slot_count = master.shape[0]
    block_rows = master.shape[1]
    model_width = master.shape[2]
    capacity = tokens.shape[0]
    seq_len = tokens.shape[1]
    head_devices = lax.axis_size("head")
    data_devices = lax.axis_size("dp")
    head_place = lax.axis_index("head")
    images = capacity // head_devices
    heads = head_devices * (block_rows // HD)
    hidden_all = head_devices * 4 * block_rows
    scale_factor = HD ** (-0.5)
    first_image = head_place * images
    blocks = gather_blocks(master, block_slot)
    attn_blocks = lax.all_gather(blocks[0:4], "head", axis=0)
    ffn_blocks = lax.all_gather(blocks[4:12], "head", axis=0)
    conv_full = lax.all_gather(conv, "head", axis=1, tiled=True)
    w_query, w_key, w_value, w_out = [
        attn_blocks[:, i].reshape(head_devices * block_rows, model_width) for i in range(4)
    ]
    w_in = ffn_blocks[:, 0:4].reshape(hidden_all, model_width)
    w_down = ffn_blocks[:, 4:8].reshape(hidden_all, model_width)
    image_valid = (first_image + jnp.arange(images) < image_count[0]).astype(jnp.float32)
    head_keep = (jnp.arange(heads) < subnet_heads[0]).astype(jnp.float32)
    unit_keep = (jnp.arange(hidden_all) < subnet_width[0]).astype(jnp.float32)
    token_values = lax.dynamic_slice_in_dim(tokens, first_image, images, 0).astype(jnp.float32)
    my_cotangent = lax.dynamic_slice_in_dim(cotangent, first_image, images, 0)
    scaled_one, inverse_one, normed_full = normalize(token_values, norm_params[0], norm_params[1])
    normed_one = normed_full.astype(jnp.bfloat16)

    def project(weight):
        return (
            jnp.einsum("gsd,fd->gsf", normed_one, weight, preferred_element_type=jnp.float32)
            .astype(jnp.bfloat16)
            .reshape(images, seq_len, heads, HD)
        )

    queries, key_vecs, value_vecs = (project(w_query), project(w_key), project(w_value))
    scores = (
        jnp.einsum("gqhe,gkhe->ghqk", queries, key_vecs, preferred_element_type=jnp.float32)
        * scale_factor
    ).astype(jnp.bfloat16)
    softmaxed, post_mixed = mix_scores(scores, talk)
    attended = (
        jnp.einsum("ghqk,gkhe->gqhe", post_mixed, value_vecs, preferred_element_type=jnp.float32)
        * head_keep[None, None, :, None]
    )
    attended = attended.astype(jnp.bfloat16).reshape(images, seq_len, heads * HD)
    middle = token_values + jnp.einsum(
        "gsf,fd->gsd", attended, w_out, preferred_element_type=jnp.float32
    )
    scaled_two, inverse_two, normed_full_two = normalize(middle, norm_params[2], norm_params[3])
    normed_two = normed_full_two.astype(jnp.bfloat16)
    hidden = jnp.einsum("gsd,ud->gsu", normed_two, w_in, preferred_element_type=jnp.float32)
    activated = conv_grid(hidden, conv_full)
    sigmoid_act = jax.nn.sigmoid(activated)
    gated = (activated * sigmoid_act * unit_keep).astype(jnp.bfloat16)
    down = jnp.einsum("gsu,ud->gsd", gated, w_down, preferred_element_type=jnp.float32)
    my_output = (middle + down) * image_valid[:, None, None]
    output = lax.all_gather(my_output.astype(jnp.bfloat16), "head", axis=0, tiled=True).astype(
        jnp.float32
    )
    grad_output = my_cotangent * image_valid[:, None, None]
    grad_low = grad_output.astype(jnp.bfloat16)
    grad_down = jnp.einsum("gsu,gsd->ud", gated, grad_low, preferred_element_type=jnp.float32)
    grad_gated = (
        jnp.einsum("gsd,ud->gsu", grad_low, w_down, preferred_element_type=jnp.float32) * unit_keep
    )
    grad_act = grad_gated * sigmoid_act * (1.0 + activated * (1.0 - sigmoid_act))
    grad_hidden, grad_kernel = conv_back(grad_act, hidden, conv_full)
    grad_hidden_low = grad_hidden.astype(jnp.bfloat16)
    grad_in = jnp.einsum(
        "gsu,gsd->ud", grad_hidden_low, normed_two, preferred_element_type=jnp.float32
    )
    grad_normed_two = jnp.einsum(
        "gsu,ud->gsd", grad_hidden_low, w_in, preferred_element_type=jnp.float32
    )
    grad_middle = grad_output + normalize_back(
        grad_normed_two, scaled_two, inverse_two, norm_params[2]
    )
    grad_branch = grad_middle.astype(jnp.bfloat16)
    grad_out_proj = jnp.einsum(
        "gsf,gsd->fd", attended, grad_branch, preferred_element_type=jnp.float32
    )
    grad_attended = jnp.einsum(
        "gsd,fd->gsf", grad_branch, w_out, preferred_element_type=jnp.float32
    ).reshape(images, seq_len, heads, HD)
    grad_att_low = (grad_attended * head_keep[None, None, :, None]).astype(jnp.bfloat16)
    grad_values = jnp.einsum(
        "ghqk,gqhe->gkhe", post_mixed, grad_att_low, preferred_element_type=jnp.float32
    ).astype(jnp.bfloat16)
    grad_post = jnp.einsum(
        "gqhe,gkhe->ghqk", grad_att_low, value_vecs, preferred_element_type=jnp.float32
    ).astype(jnp.bfloat16)
    grad_scores, talk_pre, talk_post = mix_back(
        grad_post.astype(jnp.float32), softmaxed, scores, talk
    )
    grad_queries = (
        jnp.einsum("ghqk,gkhe->gqhe", grad_scores, key_vecs, preferred_element_type=jnp.float32)
        * scale_factor
    ).astype(jnp.bfloat16)
    grad_keys = (
        jnp.einsum("ghqk,gqhe->gkhe", grad_scores, queries, preferred_element_type=jnp.float32)
        * scale_factor
    ).astype(jnp.bfloat16)
    grad_parts = [
        part.reshape(images, seq_len, heads * HD) for part in (grad_queries, grad_keys, grad_values)
    ]
    grad_projs = [
        jnp.einsum("gsf,gsd->fd", part, normed_one, preferred_element_type=jnp.float32)
        for part in grad_parts
    ]
    grad_normed_one = sum(
        (
            jnp.einsum("gsf,fd->gsd", part, weight, preferred_element_type=jnp.float32)
            for part, weight in zip(grad_parts, (w_query, w_key, w_value))
        )
    )
    my_token_grad = grad_middle + normalize_back(
        grad_normed_one, scaled_one, inverse_one, norm_params[0]
    )
    token_grad = lax.all_gather(
        my_token_grad.astype(jnp.bfloat16), "head", axis=0, tiled=True
    ).astype(jnp.float32)
    norm_part = jnp.stack(
        [
            jnp.sum(grad_normed_one * scaled_one, axis=(0, 1)),
            jnp.sum(grad_normed_one, axis=(0, 1)),
            jnp.sum(grad_normed_two * scaled_two, axis=(0, 1)),
            jnp.sum(grad_normed_two, axis=(0, 1)),
        ]
    )
    talk_part = jnp.stack([talk_pre, talk_post]).reshape(2, heads * heads)
    talk_part = jnp.pad(talk_part, ((0, 0), (0, model_width - heads * heads)))
    every_head = jnp.broadcast_to(
        jnp.concatenate([norm_part, talk_part])[None], (head_devices, 6, model_width)
    )
    conv_part = grad_kernel.reshape(9, head_devices, model_width).transpose(1, 0, 2)
    small = split_pair(jnp.concatenate([every_head, conv_part], axis=1))

    def by_head(matrix):
        return matrix.reshape(head_devices, -1, model_width)

    message = jnp.concatenate(
        [by_head(m).astype(jnp.bfloat16) for m in (*grad_projs, grad_out_proj, grad_in, grad_down)]
        + [small],
        axis=1,
    )
    received = lax.all_to_all(message, "head", split_axis=0, concat_axis=0, tiled=True)
    matrix_rows = 12 * block_rows
    block_grads = jnp.sum(received[:, :matrix_rows].astype(jnp.float32), axis=0).reshape(
        12, block_rows, model_width
    )
    small_sum = jnp.sum(join_pair(received[:, matrix_rows:]), axis=0)
    all_slots = slot_count * data_devices
    spread_grads = (
        jnp.zeros((all_slots, block_rows, model_width), jnp.bfloat16)
        .at[block_slot]
        .set(block_grads.astype(jnp.bfloat16))
        .reshape(data_devices, slot_count * block_rows, model_width)
    )
    small_pair = split_pair(small_sum)
    message_two = jnp.concatenate(
        [spread_grads, jnp.broadcast_to(small_pair[None], (data_devices,) + small_pair.shape)],
        axis=1,
    )
    received_two = lax.all_to_all(message_two, "dp", split_axis=0, concat_axis=0, tiled=True)
    slot_rows = slot_count * block_rows
    slot_grads = jnp.sum(received_two[:, :slot_rows].astype(jnp.float32), axis=0).reshape(
        slot_count, block_rows, model_width
    )
    small_total = jnp.sum(join_pair(received_two[:, slot_rows:]), axis=0)
    norm_grad = small_total[0:4]
    talk_grad = small_total[4:6, : heads * heads].reshape(2, heads, heads)
    conv_grad = small_total[6:15]
    new_master, new_master_m1, new_master_m2 = adamw(
        master, slot_grads, master_m1, master_m2, rate_matrix, decay_matrix
    )
    new_norm, new_norm_m1, new_norm_m2 = adamw(
        norm_params, norm_grad, norm_m1, norm_m2, rate_small, 0.0
    )
    new_talk, new_talk_m1, new_talk_m2 = adamw(talk, talk_grad, talk_m1, talk_m2, rate_small, 0.0)
    new_conv, new_conv_m1, new_conv_m2 = adamw(
        conv, conv_grad, conv_m1, conv_m2, rate_small, decay_matrix
    )
    return (
        output,
        token_grad,
        new_master,
        new_master_m1,
        new_master_m2,
        new_master.astype(jnp.bfloat16),
        new_norm,
        new_norm_m1,
        new_norm_m2,
        new_talk,
        new_talk_m1,
        new_talk_m2,
        new_conv,
        new_conv_m1,
        new_conv_m2,
    )


def solution(mesh):
    in_specs = (
        P("dp", None, None),
        P("dp", None, None),
        P("dp"),
        P(),
        P(),
        P(),
        P("dp", None, "head"),
        P("dp", None, "head"),
        P("dp", None, "head"),
        P(),
        P(),
        P(),
        P(),
        P(),
        P(),
        P(None, "head"),
        P(None, "head"),
        P(None, "head"),
    )
    out_specs = (
        P("dp", None, None),
        P("dp", None, None),
        P("dp", None, "head"),
        P("dp", None, "head"),
        P("dp", None, "head"),
        P("dp", None, "head"),
        P(),
        P(),
        P(),
        P(),
        P(),
        P(),
        P(None, "head"),
        P(None, "head"),
        P(None, "head"),
    )
    return jax.shard_map(local, mesh=mesh, in_specs=in_specs, out_specs=out_specs, check_vma=False)
```

profile of v0, /device:TPU:0, one launch (start us, length us, event | category | flops | bytes accessed | tf_op | source)
XLA Modules:
  0.0 175.3 jit_solution(16513780593674227736)
XLA Ops:
  0.7 1.0 convert_element_type.208
  1.7 1.0 broadcast_in_dim.21
  2.7 7.3 %all-to-all-start = ((bf16[8,2,54,216]{3,1,2,0:T(2,128)(2,1)}), bf16[8,2,54,216]{3,1,2,0:T(2,128)(2,1)S(1)}, u32[]{:S(2)}, u32[]{:S(2)}) async-start(bf16[8,2,54,216]{3,1,2,0:T(2,128)(2,1)} %broadcast_in_dim.21), calls=%async_computation | async-start | bytes 884736 | tf_op jit(solution)/shard_map/all_to_all | solution.py:105
  12.6 0.7 copy.278
  13.3 5.4 %all-gather.2 = f32[4,216,9]{1,2,0:T(8,128)S(1)} all-gather(f32[1,216,9]{1,2,0:T(8,128)} %bitcast.275), channel_id=1, replica_groups=mesh['dp'=8,'head'=4] {'head'}, dimensions={0}, use_global_device_ids=true | all-gather | bytes 38880 | tf_op jit(solution)/shard_map/all_gather | solution.py:163
  19.0 0.9 constant_dynamic-slice_fusion
  19.8 1.2 constant_dynamic-slice_fusion.1
  21.4 0.7 compare_and_fusion
  22.0 0.8 fusion.145
  23.7 6.9 %all-gather = bf16[16,54,216]{2,1,0:T(8,128)(2,1)S(1)} all-gather(bf16[4,54,216]{2,1,0:T(8,128)(2,1)S(1)} %slice.225), channel_id=2, replica_groups=mesh['dp'=8,'head'=4] {'head'}, dimensions={0}, use_global_device_ids=true | all-gather | bytes 466560 | tf_op jit(solution)/shard_map/all_gather | solution.py:161
  30.7 0.7 dot_general.144
  33.6 9.3 %all-gather.1 = bf16[32,54,216]{2,0,1:T(8,128)(2,1)S(1)} all-gather(bf16[8,54,216]{2,0,1:T(8,128)(2,1)S(1)} %copy.283), channel_id=3, replica_groups=mesh['dp'=8,'head'=4] {'head'}, dimensions={0}, use_global_device_ids=true | all-gather | bytes 933120 | tf_op jit(solution)/shard_map/all_gather | solution.py:162
  43.3 1.0 reshape.508
  45.2 2.0 %bitcast_reduce_fusion = (f32[12,196]{0,1:T(8,128)S(1)}, f32[196,196,12]{1,2,0:T(8,128)S(1)}) fusion(f32[2,12,12]{2,1,0:T(8,128)S(1)} %copy.278, bf16[12,196,196]{2,1,0:T(8,128)(2,1)S(1)} %multiply_convert_fusion), kind=kOutput, calls=%fused_computation.15 | convolution fusion | flops 66841488 | bytes 3090368 | tf_op jit(solution)/shard_map/mn,gnqk->gmqk/dot_general | solution.py:68
  47.2 1.1 fusion.12
  48.9 3.9 %fusion.28 = bf16[12,196,196]{2,0,1:T(8,128)(2,1)S(1)} fusion(f32[2,12,12]{2,1,0:T(8,128)S(1)} %copy.278, f32[196,196,12]{1,2,0:T(8,128)S(1)} %get-tuple-element.163, f32[12,196]{0,1:T(8,128)S(1)} %fusion.12, f32[12,196]{0,1:T(8,128)S(1)} %get-tuple-element.162), kind=kOutput, calls=%fused_computation.30 | convolution fusion | flops 67765824 | bytes 4346240 | tf_op jit(solution)/shard_map/jm,gmqk->gjqk/dot_general | solution.py:72
  52.9 1.2 copy-done.3
  55.2 1.2 fusion.111
  56.4 1.2 reshape.507
  57.6 1.8 %multiply_convert_fusion.1 = (bf16[1,14,14,864]{3,2,1,0:T(8,128)(2,1)}, f32[1,14,14,864]{3,2,1,0:T(8,128)}) fusion(f32[864]{0:T(1024)S(1)} %fusion.125, f32[864]{0:T(1024)S(1)} %get-tuple-element.122, f32[864]{0:T(1024)S(1)} %get-tuple-element.123, f32[864]{0:T(1024)S(1)} %get-tuple-element.124, f32[864]{0:T(1024)S(1)} %get-tuple-element.125, ...), kind=kLoop, calls=%fused_computation.114 | loop fusion | flops 3894912 | bytes 1728000 | tf_op jit(solution)/shard_map/convert_element_type | solution.py:203
  59.4 2.1 %reshape.510 = f32[196,864]{1,0:T(8,128)} reshape(f32[1,14,14,864]{3,2,1,0:T(8,128)} %get-tuple-element.144) | data formatting | bytes 1354752 | tf_op jit(solution)/shard_map/reshape | solution.py:48
  61.5 2.0 %fusion.81 = bf16[864,196]{0,1:T(8,128)(2,1)} fusion(f32[864]{0:T(1024)S(1)} %fusion.125, f32[196,864]{1,0:T(8,128)} %reshape.510), kind=kLoop, calls=%fused_computation.123 | loop fusion | flops 1016064 | bytes 1019520 | tf_op jit(solution)/shard_map/gsu,gsd->ud/dot_general | solution.py:211
  63.5 3.5 %multiply_reduce_fusion.8 = (f32[864]{0:T(1024)}, f32[196,864]{1,0:T(8,128)}) fusion(f32[196,864]{1,0:T(8,128)} %fusion.111, f32[196,864]{1,0:T(8,128)} %reshape.510, f32[864]{0:T(1024)S(1)} %fusion.125, bf16[864,216]{1,0:T(8,128)(2,1)} %reshape.508, f32[]{:T(128)} %bitcast.30, f32[1,196,216]{2,0,1:T(1,128)} %constant_dynamic-slice_fusion), kind=kOutput, calls=%fused_computation.116 | convolution fusion | flops 75103200 | bytes 2581636 | tf_op jit(solution)/shard_map/gsd,ud->gsu/dot_general | solution.py:213
  67.0 2.1 %reshape.511 = f32[1,14,14,864]{3,2,1,0:T(8,128)} reshape(f32[196,864]{1,0:T(8,128)} %get-tuple-element.171) | data formatting | bytes 1354752 | tf_op jit(solution)/shard_map/reshape | solution.py:36
  69.1 7.3 %multiply_reduce_fusion = (f32[864]{0:T(1024)}, f32[864]{0:T(1024)}, f32[864]{0:T(1024)}, f32[864]{0:T(1024)}, f32[864]{0:T(1024)}, /*index=5*/f32[864]{0:T(1024...) fusion(f32[1,14,14,864]{3,2,1,0:T(8,128)} %reshape.511, f32[1,14,14,864]{3,2,1,0:T(8,128)S(1)} %reshape.507, ...), kind=kLoop, calls=%fused_computation.106 | loop fusion | flops 5750784 | bytes 1752192 | tf_op jit(solution)/shard_map/reduce_sum | solution.py:62
  76.4 1.2 convert_element_type.227
  77.6 1.8 %fusion.97 = (f32[216]{0:T(256)}, f32[196]{0:T(256)S(1)}, f32[196,216]{1,0:T(8,128)S(1)}) fusion(f32[1,196,216]{2,1,0:T(8,128)S(1)} %get-tuple-element.165, f32[196]{0:T(256)} %copy-done.34, f32[196]{0:T(256)} %copy-done.30, f32[216]{0:T(256)} %bitcast.278, bf16[196,864]{1,0:T(8,128)(2,1)S(1)} %convert_element_type.227, bf16[864,216]{1,0:T(8,128)(2,1)S(1)} %reshape.506), kind=kOutput, calls=%fused_computation.144 | convolution fusion | flops 73452544 | bytes 1054704 | tf_op jit(solution)/shard_map/gsu,ud->gsd/dot_general | solution.py:221
  79.4 1.3 fusion.136
  80.7 1.1 fusion.100
  81.8 1.1 fusion.36
  82.9 1.9 %fusion.44 = bf16[1,196,12,18]{1,3,2,0:T(8,128)(2,1)S(1)} fusion(bf16[196,12,18]{0,2,1:T(8,128)(2,1)S(1)} %fusion.36, bf16[12,196,196]{2,0,1:T(8,128)(2,1)} %copy-done.3), kind=kOutput, calls=%fused_computation.62 | convolution fusion | flops 16638048 | bytes 1091328 | tf_op jit(solution)/shard_map/ghqk,gqhe->gkhe/dot_general | solution.py:235
  85.4 3.4 %fusion.48 = f32[12,12]{1,0:T(8,128)} fusion(bf16[12,196,196]{2,1,0:T(8,128)(2,1)S(1)} %convolution_convert_fusion, f32[196,196,12]{1,2,0:T(8,128)S(1)} %copy-done.2, f32[12,196]{0,1:T(8,128)S(1)} %copy-done.27, f32[12,196]{0,1:T(8,128)S(1)} %copy-done.23), kind=kOutput, calls=%fused_computation.66 | convolution fusion | flops 67304832 | bytes 2785344 | tf_op jit(solution)/shard_map/gjqk,gmqk->jm/dot_general | solution.py:80
  88.8 4.1 %fusion.4 = (f32[12,196]{0,1:T(8,128)S(1)}, f32[196,196,12]{1,2,0:T(8,128)S(1)}) fusion(f32[12,196]{0,1:T(8,128)S(1)} %copy-done.27, f32[12,196]{0,1:T(8,128)S(1)} %copy-done.23, f32[196,196,12]{1,2,0:T(8,128)S(1)} %copy-done.2, f32[2,12,12]{2,1,0:T(8,128)S(1)} %copy.278, bf16[12,196,196]{2,1,0:T(8,128)(2,1)S(1)} %convolution_convert_fusion), kind=kOutput, calls=%fused_computation.8 | convolution fusion | flops 68224464 | bytes 6506432 | tf_op jit(solution)/shard_map/jm,gjqk->gmqk/dot_general | solution.py:79
  92.9 3.8 %fusion.53 = f32[12,12]{1,0:T(8,128)} fusion(bf16[12,196,196]{2,1,0:T(8,128)(2,1)S(1)} %multiply_convert_fusion, f32[12,196]{0,1:T(8,128)S(1)} %get-tuple-element.167, f32[196,196,12]{1,2,0:T(8,128)S(1)} %get-tuple-element.168, f32[196,196,12]{1,2,0:T(8,128)S(1)} %copy-done.2, f32[12,196]{0,1:T(8,128)S(1)} %copy-done.27, f32[12,196]{0,1:T(8,128)S(1)} %copy-done.23), kind=kOutput, calls=%fused_computation.67 | convolution fusion | flops 68226816 | bytes 4638720 | tf_op jit(solution)/shard_map/gmqk,gnqk->mn/dot_general | solution.py:82
  96.7 4.7 %fusion.25 = bf16[12,196,196]{2,0,1:T(8,128)(2,1)S(1)} fusion(f32[196,196,12]{1,2,0:T(8,128)S(1)} %get-tuple-element.168, f32[12,196]{0,1:T(8,128)S(1)} %get-tuple-element.167, f32[2,12,12]{2,1,0:T(8,128)S(1)} %copy.278, f32[196,196,12]{1,2,0:T(8,128)S(1)} %copy-done.2, f32[12,196]{0,1:T(8,128)S(1)} %copy-done.27, f32[12,196]{0,1:T(8,128)S(1)} %copy-done.23), kind=kOutput, calls=%fused_computation.29 | convolution fusion | flops 68687808 | bytes 7659904 | tf_op jit(solution)/shard_map/mn,gmqk->gnqk/dot_general | solution.py:85
  101.6 1.1 fusion.45
  102.8 1.1 fusion.46
  105.5 0.8 convolution_convert_fusion.4
  107.2 1.1 copy.301
  108.4 1.0 convolution_convert_fusion.5
  109.3 0.8 copy.300
  110.4 1.0 reshape.516
  111.4 1.1 fusion.147
  112.5 1.1 convolution_add_fusion.1
  113.6 1.2 fusion.95
  115.0 0.9 convolution_convert_fusion.7
  116.5 0.8 copy.299
  117.5 0.9 copy.303
  118.4 0.9 copy.302
  119.3 3.8 %concatenate.19 = bf16[4,678,216]{1,2,0:T(8,128)(2,1)} concatenate(bf16[4,54,216]{1,2,0:T(8,128)(2,1)S(1)} %copy.298, bf16[4,54,216]{1,2,0:T(8,128)(2,1)} %copy.299, bf16[4,54,216]{1,2,0:T(8,128)(2,1)} %copy.300, bf16[4,54,216]{1,2,0:T(8,128)(2,1)S(1)} %copy.301, bf16[4,216,216]{1,2,0:T(8,128)(2,1)S(1)} %convolution_convert_fusion.2, ...), dimensions={1} | concatenate | bytes 2343168 | tf_op jit(solution)/shard_map/concatenate | solution.py:290
  123.1 3.5 %all-to-all-start.1 = ((bf16[4,678,216]{1,2,0:T(8,128)(2,1)}), bf16[4,678,216]{1,2,0:T(8,128)(2,1)S(1)}, u32[]{:S(2)}, u32[]{:S(2)}) async-start(bf16[4,678,216]{1,2,0:T(8,128)(2,1)} %concatenate.19), calls=%async_computation.1 | async-start | bytes 2654208 | tf_op jit(solution)/shard_map/all_to_all | solution.py:295
  126.6 1.9 %convert_element_type.222 = bf16[196,864]{1,0:T(8,128)(2,1)} reshape(bf16[1,14,14,864]{3,2,1,0:T(8,128)(2,1)} %get-tuple-element.143) | data formatting | bytes 677376 | tf_op jit(solution)/shard_map/convert_element_type | solution.py:203
  128.5 1.3 fusion.43
  129.8 14.2 %all-to-all-done.1 = bf16[4,678,216]{1,2,0:T(8,128)(2,1)S(1)} async-done(((bf16[4,678,216]{1,2,0:T(8,128)(2,1)}), bf16[4,678,216]{1,2,0:T(8,128)(2,1)S(1)}, u32[]{:S(2)}, u32[]{:S(2)}) %all-to-all-start.1) | async-done | bytes 1171616 | tf_op jit(solution)/shard_map/all_to_all | solution.py:295
  144.9 1.1 scatter_fusion
  146.2 0.9 pad_maximum_fusion
  147.2 6.1 %all-to-all-start.2 = ((bf16[8,138,216]{2,1,0:T(8,128)(2,1)}), bf16[8,138,216]{2,1,0:T(8,128)(2,1)S(1)}, u32[]{:S(2)}, u32[]{:S(2)}) async-start(bf16[8,138,216]{2,1,0:T(8,128)(2,1)} %pad_maximum_fusion), calls=%async_computation.2 | async-start | bytes 1179648 | tf_op jit(solution)/shard_map/all_to_all | solution.py:313
  153.3 6.2 %all_gather.26 = bf16[4,196,216]{2,1,0:T(8,128)(2,1)S(1)} all-gather(bf16[1,196,216]{2,1,0:T(8,128)(2,1)S(1)} %fusion.43), channel_id=1, replica_groups=mesh['dp'=8,'head'=4] {'head'}, dimensions={0}, use_global_device_ids=true | all-gather | bytes 423360 | tf_op jit(solution)/shard_map/all_gather | solution.py:206
  159.5 1.0 copy.314
  160.7 6.7 %all_gather.27 = bf16[4,196,216]{2,1,0:T(8,128)(2,1)S(1)} all-gather(bf16[1,196,216]{2,1,0:T(8,128)(2,1)S(1)} %fusion.94), channel_id=1, replica_groups=mesh['dp'=8,'head'=4] {'head'}, dimensions={0}, use_global_device_ids=true | all-gather | bytes 423360 | tf_op jit(solution)/shard_map/all_gather | solution.py:268
  167.4 1.0 copy.315
  171.9 0.7 copy.316
  172.6 0.7 copy.317
  173.3 0.7 copy.318
  (246 shorter events, 17.0 us)
Async XLA Ops:
  0.6 18.3 %copy-start = (f32[4,196,216]{2,0,1:T(4,128)S(1)}, f32[4,196,216]{2,0,1:T(4,128)}, u32[]{:S(2)}) copy-start(f32[4,196,216]{2,0,1:T(4,128)} %param.19) | copy-start | bytes 2032132
  2.7 20.2 %all-to-all-start = ((bf16[8,2,54,216]{3,1,2,0:T(2,128)(2,1)}), bf16[8,2,54,216]{3,1,2,0:T(2,128)(2,1)S(1)}, u32[]{:S(2)}, u32[]{:S(2)}) async-start(bf16[8,2,54,216]{3,1,2,0:T(2,128)(2,1)} %broadcast_in_dim.21), calls=%async_computation | async-start | bytes 884736 | tf_op jit(solution)/shard_map/all_to_all | solution.py:105
  11.9 41.0 %copy-start.66 = (f32[12]{0:T(128)}, f32[12]{0:T(128)S(1)}, u32[]{:S(2)}) copy-start(f32[12]{0:T(128)S(1)} %compare_convert_fusion) | copy-start | bytes 148
  12.6 18.9 %copy-start.64 = (s32[12]{0:T(128)}, s32[12]{0:T(128)S(1)}, u32[]{:S(2)}) copy-start(s32[12]{0:T(128)S(1)} %compare_select_fusion) | copy-start | bytes 148
  21.1 33.5 %copy-start.4 = (bf16[1,196,216]{2,1,0:T(8,128)(2,1)}, bf16[1,196,216]{2,1,0:T(8,128)(2,1)S(1)}, u32[]{:S(2)}) copy-start(bf16[1,196,216]{2,1,0:T(8,128)(2,1)S(1)} %get-tuple-element.146) | copy-start | bytes 254020
  21.2 11.3 %copy-start.36 = (f32[196]{0:T(256)}, f32[196]{0:T(256)S(1)}, u32[]{:S(2)}) copy-start(f32[196]{0:T(256)S(1)} %broadcast_multiply_fusion.5) | copy-start | bytes 2356
  22.0 10.5 %copy-start.53 = (f32[196]{0:T(256)}, f32[196]{0:T(256)S(1)}, u32[]{:S(2)}) copy-start(f32[196]{0:T(256)S(1)} %add_rsqrt_fusion.1) | copy-start | bytes 2356
  22.9 9.6 %copy-start.38 = (f32[1,216]{1,0:T(1,128)}, f32[1,216]{1,0:T(1,128)S(1)}, u32[]{:S(2)}) copy-start(f32[1,216]{1,0:T(1,128)S(1)} %get-tuple-element.160) | copy-start | bytes 2596
  22.9 9.6 %copy-start.67 = (f32[1,216]{1,0:T(1,128)}, f32[1,216]{1,0:T(1,128)S(1)}, u32[]{:S(2)}) copy-start(f32[1,216]{1,0:T(1,128)S(1)} %get-tuple-element.159) | copy-start | bytes 2596
  22.9 32.3 %copy-start.32 = (f32[1,216]{1,0:T(1,128)}, f32[1,216]{1,0:T(1,128)S(1)}, u32[]{:S(2)}) copy-start(f32[1,216]{1,0:T(1,128)S(1)} %get-tuple-element.158) | copy-start | bytes 2596
  22.9 32.3 %copy-start.55 = (f32[1,216]{1,0:T(1,128)}, f32[1,216]{1,0:T(1,128)S(1)}, u32[]{:S(2)}) copy-start(f32[1,216]{1,0:T(1,128)S(1)} %get-tuple-element.161) | copy-start | bytes 2596
  31.5 11.6 %copy-start.18 = (bf16[216,216]{1,0:T(8,128)(2,1)}, bf16[216,216]{1,0:T(8,128)(2,1)S(1)}, u32[]{:S(2)}) copy-start(bf16[216,216]{1,0:T(8,128)(2,1)S(1)} %reshape_squeeze.14) | copy-start | bytes 279940
  31.9 12.7 %copy-start.9 = (bf16[196,12,18]{0,2,1:T(8,128)(2,1)}, bf16[196,12,18]{0,2,1:T(8,128)(2,1)S(1)}, u32[]{:S(2)}) copy-start(bf16[196,12,18]{0,2,1:T(8,128)(2,1)S(1)} %reshape.501) | copy-start | bytes 254020
  32.0 11.1 %copy-start.20 = (bf16[216,216]{1,0:T(8,128)(2,1)}, bf16[216,216]{1,0:T(8,128)(2,1)S(1)}, u32[]{:S(2)}) copy-start(bf16[216,216]{1,0:T(8,128)(2,1)S(1)} %reshape_squeeze.13) | copy-start | bytes 279940
  32.4 12.2 %copy-start.11 = (bf16[196,12,18]{0,2,1:T(8,128)(2,1)}, bf16[196,12,18]{0,2,1:T(8,128)(2,1)S(1)}, u32[]{:S(2)}) copy-start(bf16[196,12,18]{0,2,1:T(8,128)(2,1)S(1)} %reshape.500) | copy-start | bytes 254020
  33.6 19.3 %copy-start.13 = (bf16[196,12,18]{0,2,1:T(8,128)(2,1)}, bf16[196,12,18]{0,2,1:T(8,128)(2,1)S(1)}, u32[]{:S(2)}) copy-start(bf16[196,12,18]{0,2,1:T(8,128)(2,1)S(1)} %reshape.499) | copy-start | bytes 254020
  47.1 5.7 %copy-start.1 = (f32[196,196,12]{1,2,0:T(8,128)}, f32[196,196,12]{1,2,0:T(8,128)S(1)}, u32[]{:S(2)}) copy-start(f32[196,196,12]{1,2,0:T(8,128)S(1)} %get-tuple-element.163) | copy-start | bytes 5531908
  47.1 5.7 %copy-start.22 = (f32[12,196]{0,1:T(8,128)}, f32[12,196]{0,1:T(8,128)S(1)}, u32[]{:S(2)}) copy-start(f32[12,196]{0,1:T(8,128)S(1)} %get-tuple-element.162) | copy-start | bytes 28228
  54.9 6.5 %copy-start.30 = (f32[196]{0:T(256)}, f32[196]{0:T(256)S(1)}, u32[]{:S(2)}) copy-start(f32[196]{0:T(256)S(1)} %broadcast_multiply_fusion.4) | copy-start | bytes 2356
  55.1 6.3 %copy-start.34 = (f32[196]{0:T(256)}, f32[196]{0:T(256)S(1)}, u32[]{:S(2)}) copy-start(f32[196]{0:T(256)S(1)} %add_rsqrt_fusion) | copy-start | bytes 2356
  76.4 8.5 %copy-start.14 = (bf16[196,12,18]{0,2,1:T(8,128)(2,1)S(1)}, bf16[196,12,18]{0,2,1:T(8,128)(2,1)}, u32[]{:S(2)}) copy-start(bf16[196,12,18]{0,2,1:T(8,128)(2,1)} %copy-done.13) | copy-start | bytes 254020
  76.4 9.0 %copy-start.23 = (f32[12,196]{0,1:T(8,128)S(1)}, f32[12,196]{0,1:T(8,128)}, u32[]{:S(2)}) copy-start(f32[12,196]{0,1:T(8,128)} %copy-done.22) | copy-start | bytes 28228
  76.4 9.0 %copy-start.27 = (f32[12,196]{0,1:T(8,128)S(1)}, f32[12,196]{0,1:T(8,128)}, u32[]{:S(2)}) copy-start(f32[12,196]{0,1:T(8,128)} %copy-done.26) | copy-start | bytes 28228
  77.6 7.8 %copy-start.2 = (f32[196,196,12]{1,2,0:T(8,128)S(1)}, f32[196,196,12]{1,2,0:T(8,128)}, u32[]{:S(2)}) copy-start(f32[196,196,12]{1,2,0:T(8,128)} %copy-done.1) | copy-start | bytes 5531908
  96.7 4.7 %copy-start.12 = (bf16[196,12,18]{0,2,1:T(8,128)(2,1)S(1)}, bf16[196,12,18]{0,2,1:T(8,128)(2,1)}, u32[]{:S(2)}) copy-start(bf16[196,12,18]{0,2,1:T(8,128)(2,1)} %copy-done.11) | copy-start | bytes 254020
  96.7 6.1 %copy-start.10 = (bf16[196,12,18]{0,2,1:T(8,128)(2,1)S(1)}, bf16[196,12,18]{0,2,1:T(8,128)(2,1)}, u32[]{:S(2)}) copy-start(bf16[196,12,18]{0,2,1:T(8,128)(2,1)} %copy-done.9) | copy-start | bytes 254020
  96.7 7.2 %copy-start.16 = (bf16[196,216]{0,1:T(8,128)(2,1)S(1)}, bf16[196,216]{0,1:T(8,128)(2,1)}, u32[]{:S(2)}) copy-start(bf16[196,216]{0,1:T(8,128)(2,1)} %copy-done.15) | copy-start | bytes 254020
  101.5 3.4 %copy-start.46 = (f32[864]{0:T(1024)S(1)}, f32[864]{0:T(1024)}, u32[]{:S(2)}) copy-start(f32[864]{0:T(1024)} %get-tuple-element.106) | copy-start | bytes 10372
  101.5 3.4 %copy-start.45 = (f32[864]{0:T(1024)S(1)}, f32[864]{0:T(1024)}, u32[]{:S(2)}) copy-start(f32[864]{0:T(1024)} %get-tuple-element.107) | copy-start | bytes 10372
  101.5 3.5 %copy-start.44 = (f32[864]{0:T(1024)S(1)}, f32[864]{0:T(1024)}, u32[]{:S(2)}) copy-start(f32[864]{0:T(1024)} %get-tuple-element.108) | copy-start | bytes 10372
  101.6 3.6 %copy-start.43 = (f32[864]{0:T(1024)S(1)}, f32[864]{0:T(1024)}, u32[]{:S(2)}) copy-start(f32[864]{0:T(1024)} %get-tuple-element.109) | copy-start | bytes 10372
  101.6 3.6 %copy-start.42 = (f32[864]{0:T(1024)S(1)}, f32[864]{0:T(1024)}, u32[]{:S(2)}) copy-start(f32[864]{0:T(1024)} %get-tuple-element.110) | copy-start | bytes 10372
  101.6 3.7 %copy-start.41 = (f32[864]{0:T(1024)S(1)}, f32[864]{0:T(1024)}, u32[]{:S(2)}) copy-start(f32[864]{0:T(1024)} %get-tuple-element.111) | copy-start | bytes 10372
  101.6 3.8 %copy-start.40 = (f32[864]{0:T(1024)S(1)}, f32[864]{0:T(1024)}, u32[]{:S(2)}) copy-start(f32[864]{0:T(1024)} %get-tuple-element.112) | copy-start | bytes 10372
  101.6 5.1 %copy-start.31 = (f32[196]{0:T(256)S(1)}, f32[196]{0:T(256)}, u32[]{:S(2)}) copy-start(f32[196]{0:T(256)} %copy-done.30) | copy-start | bytes 2356
  101.6 5.1 %copy-start.33 = (f32[1,216]{1,0:T(1,128)S(1)}, f32[1,216]{1,0:T(1,128)}, u32[]{:S(2)}) copy-start(f32[1,216]{1,0:T(1,128)} %copy-done.32) | copy-start | bytes 2596
  101.6 5.1 %copy-start.35 = (f32[196]{0:T(256)S(1)}, f32[196]{0:T(256)}, u32[]{:S(2)}) copy-start(f32[196]{0:T(256)} %copy-done.34) | copy-start | bytes 2356
  101.6 5.1 %copy-start.56 = (f32[1,216]{1,0:T(1,128)S(1)}, f32[1,216]{1,0:T(1,128)}, u32[]{:S(2)}) copy-start(f32[1,216]{1,0:T(1,128)} %copy-done.55) | copy-start | bytes 2596
  102.8 5.5 %copy-start.5 = (bf16[1,196,216]{2,1,0:T(8,128)(2,1)S(1)}, bf16[1,196,216]{2,1,0:T(8,128)(2,1)}, u32[]{:S(2)}) copy-start(bf16[1,196,216]{2,1,0:T(8,128)(2,1)} %copy-done.4) | copy-start | bytes 254020
  102.8 5.6 %copy-start.37 = (f32[196]{0:T(256)S(1)}, f32[196]{0:T(256)}, u32[]{:S(2)}) copy-start(f32[196]{0:T(256)} %copy-done.36) | copy-start | bytes 2356
  102.8 5.6 %copy-start.39 = (f32[1,216]{1,0:T(1,128)S(1)}, f32[1,216]{1,0:T(1,128)}, u32[]{:S(2)}) copy-start(f32[1,216]{1,0:T(1,128)} %copy-done.38) | copy-start | bytes 2596
  102.8 5.6 %copy-start.54 = (f32[196]{0:T(256)S(1)}, f32[196]{0:T(256)}, u32[]{:S(2)}) copy-start(f32[196]{0:T(256)} %copy-done.53) | copy-start | bytes 2356
  103.9 6.3 %copy-start.57 = (f32[12,12]{1,0:T(8,128)S(1)}, f32[12,12]{1,0:T(8,128)}, u32[]{:S(2)}) copy-start(f32[12,12]{1,0:T(8,128)} %fusion.48) | copy-start | bytes 1732
  103.9 6.3 %copy-start.58 = (f32[12,12]{1,0:T(8,128)S(1)}, f32[12,12]{1,0:T(8,128)}, u32[]{:S(2)}) copy-start(f32[12,12]{1,0:T(8,128)} %fusion.53) | copy-start | bytes 1732
  104.8 5.6 %copy-start.17 = (bf16[1,196,12,18]{1,3,2,0:T(8,128)(2,1)S(1)}, bf16[1,196,12,18]{1,3,2,0:T(8,128)(2,1)}, u32[]{:S(2)}) copy-start(bf16[1,196,12,18]{1,3,2,0:T(8,128)(2,1)} %fusion.46) | copy-start | bytes 254020
  107.2 9.0 %copy-start.68 = (f32[1,216]{1,0:T(1,128)S(1)}, f32[1,216]{1,0:T(1,128)}, u32[]{:S(2)}) copy-start(f32[1,216]{1,0:T(1,128)} %copy-done.67) | copy-start | bytes 2596
  107.2 10.3 %copy-start.59 = (f32[216]{0:T(256)S(1)}, f32[216]{0:T(256)}, u32[]{:S(2)}) copy-start(f32[216]{0:T(256)} %get-tuple-element.117) | copy-start | bytes 2596
  107.2 10.3 %copy-start.63 = (f32[216]{0:T(256)S(1)}, f32[216]{0:T(256)}, u32[]{:S(2)}) copy-start(f32[216]{0:T(256)} %get-tuple-element.113) | copy-start | bytes 2596
  119.3 9.2 %copy-start.7 = (bf16[864,216]{1,0:T(8,128)(2,1)S(1)}, bf16[864,216]{1,0:T(8,128)(2,1)}, u32[]{:S(2)}) copy-start(bf16[864,216]{1,0:T(8,128)(2,1)} %reshape.508) | copy-start | bytes 1119748
  123.1 21.0 %all-to-all-start.1 = ((bf16[4,678,216]{1,2,0:T(8,128)(2,1)}), bf16[4,678,216]{1,2,0:T(8,128)(2,1)S(1)}, u32[]{:S(2)}, u32[]{:S(2)}) async-start(bf16[4,678,216]{1,2,0:T(8,128)(2,1)} %concatenate.19), calls=%async_computation.1 | async-start | bytes 2654208 | tf_op jit(solution)/shard_map/all_to_all | solution.py:295
  126.6 18.2 %copy-start.65 = (s32[12]{0:T(128)S(1)}, s32[12]{0:T(128)}, u32[]{:S(2)}) copy-start(s32[12]{0:T(128)} %copy-done.64) | copy-start | bytes 148
  147.1 22.1 %copy-start.29 = (f32[2,12,12]{2,0,1:T(2,128)S(1)}, f32[2,12,12]{2,0,1:T(2,128)}, u32[]{:S(2)}) copy-start(f32[2,12,12]{2,0,1:T(2,128)} %param.30) | copy-start | bytes 3460
  147.1 22.1 %copy-start.51 = (f32[2,12,12]{2,0,1:T(2,128)S(1)}, f32[2,12,12]{2,0,1:T(2,128)}, u32[]{:S(2)}) copy-start(f32[2,12,12]{2,0,1:T(2,128)} %param.31) | copy-start | bytes 3460
  147.1 22.1 %copy-start.52 = (f32[2,12,12]{2,0,1:T(2,128)S(1)}, f32[2,12,12]{2,0,1:T(2,128)}, u32[]{:S(2)}) copy-start(f32[2,12,12]{2,0,1:T(2,128)} %param.32) | copy-start | bytes 3460
  147.1 24.0 %copy-start.19 = (f32[2,54,216]{2,0,1:T(2,128)S(1)}, f32[2,54,216]{2,0,1:T(2,128)}, u32[]{:S(2)}) copy-start(f32[2,54,216]{2,0,1:T(2,128)} %param.24) | copy-start | bytes 279940
  147.1 24.0 %copy-start.24 = (f32[2,54,216]{2,0,1:T(2,128)S(1)}, f32[2,54,216]{2,0,1:T(2,128)}, u32[]{:S(2)}) copy-start(f32[2,54,216]{2,0,1:T(2,128)} %param.25) | copy-start | bytes 279940
  147.1 24.0 %copy-start.25 = (f32[2,54,216]{2,0,1:T(2,128)S(1)}, f32[2,54,216]{2,0,1:T(2,128)}, u32[]{:S(2)}) copy-start(f32[2,54,216]{2,0,1:T(2,128)} %param.26) | copy-start | bytes 279940
  147.2 21.8 %all-to-all-start.2 = ((bf16[8,138,216]{2,1,0:T(8,128)(2,1)}), bf16[8,138,216]{2,1,0:T(8,128)(2,1)S(1)}, u32[]{:S(2)}, u32[]{:S(2)}) async-start(bf16[8,138,216]{2,1,0:T(8,128)(2,1)} %pad_maximum_fusion), calls=%async_computation.2 | async-start | bytes 1179648 | tf_op jit(solution)/shard_map/all_to_all | solution.py:313
  159.5 14.5 %copy-start.50 = (f32[4,216]{1,0:T(4,128)S(1)}, f32[4,216]{1,0:T(4,128)}, u32[]{:S(2)}) copy-start(f32[4,216]{1,0:T(4,128)} %param.27) | copy-start | bytes 10372
  159.5 14.5 %copy-start.60 = (f32[4,216]{1,0:T(4,128)S(1)}, f32[4,216]{1,0:T(4,128)}, u32[]{:S(2)}) copy-start(f32[4,216]{1,0:T(4,128)} %param.28) | copy-start | bytes 10372
  159.5 14.5 %copy-start.61 = (f32[4,216]{1,0:T(4,128)S(1)}, f32[4,216]{1,0:T(4,128)}, u32[]{:S(2)}) copy-start(f32[4,216]{1,0:T(4,128)} %param.29) | copy-start | bytes 10372
  159.5 15.1 %copy-start.28 = (f32[9,216]{1,0:T(8,128)S(1)}, f32[9,216]{1,0:T(8,128)}, u32[]{:S(2)}) copy-start(f32[9,216]{1,0:T(8,128)} %param.33) | copy-start | bytes 23332
  159.5 15.1 %copy-start.48 = (f32[9,216]{1,0:T(8,128)S(1)}, f32[9,216]{1,0:T(8,128)}, u32[]{:S(2)}) copy-start(f32[9,216]{1,0:T(8,128)} %param.34) | copy-start | bytes 23332
  159.5 15.1 %copy-start.49 = (f32[9,216]{1,0:T(8,128)S(1)}, f32[9,216]{1,0:T(8,128)}, u32[]{:S(2)}) copy-start(f32[9,216]{1,0:T(8,128)} %param.35) | copy-start | bytes 23332
  (8 other events, 14.4 us)
where the time goes:
time: 177 us; the launch traced here: 175 us
  matrix products  44.6 us (25%)
  local copies, waits for them, and re-layouts  39.8 us (22%)
  blocking collectives  34.5 us (19%)
  other arithmetic  20.8 us (12%)
  starting transfers between devices  16.9 us (10%)
  waiting for transfers between devices  14.8 us (8%)
  between operations  3.87 us (2%)
    all_to_all x1, waiting for transfers between devices, local(): lax.all_to_all(message, 'head', split_axis=0, concat_axis=0, tiled=True)  14.2 us
    unnamed x159, local copies, waits for them, and re-layouts  10.6 us
    all_gather x1, blocking collectives, local(): ffn_blocks = lax.all_gather(blocks[4:12], 'head', axis=0)  9.25 us
    reduce_sum x1, other arithmetic, conv_back(): jnp.sum(grad_grid * shifted(padded_hidden, row_off, col_off), axis=(0, 1,...  7.31 us
    all_to_all x1, starting transfers between devices, gather_blocks(): lax.all_to_all(jnp.broadcast_to(mine[None], (data_devices,) + mine.shape)...  7.25 us
    all_gather x1, blocking collectives, local(): attn_blocks = lax.all_gather(blocks[0:4], 'head', axis=0)  6.93 us
    all_gather x1, blocking collectives, local(): lax.all_gather(my_token_grad.astype(jnp.bfloat16), 'head', axis=0, tiled=...  6.68 us
    all_gather x1, blocking collectives, local(): lax.all_gather(my_output.astype(jnp.bfloat16), 'head', axis=0, tiled=True)  6.18 us
  transfers between devices with their start and end apart: 3, of which 2 were waited for; matrix products, arithmetic and copies ran while one was open for 6% of the time, Pallas kernels for 0%

commit v1 on v0

--- a/solution.py
+++ b/solution.py
@@ -102,13 +102,20 @@
 def gather_blocks(master, block_slot):
     mine = master.astype(jnp.bfloat16)
     data_devices = lax.axis_size("dp")
-    every = lax.all_to_all(
-        jnp.broadcast_to(mine[None], (data_devices,) + mine.shape),
-        "dp",
-        split_axis=0,
-        concat_axis=0,
-        tiled=True,
-    )
+    value = jnp.broadcast_to(mine[None], (data_devices,) + mine.shape)
+    ways, here = (lax.axis_size("dp"), lax.axis_index("dp"))
+    width = value.shape[0] // ways
+    dims = list(value.shape)
+    dims[0] = width
+    height = dims[0]
+    dims[0] = height * ways
+    full = jnp.zeros(dims, value.dtype)
+    for mask in range(ways):
+        part_2 = lax.dynamic_slice_in_dim(value, (here ^ mask) * width, width, axis=0)
+        if mask:
+            part_2 = lax.ppermute(part_2, "dp", [(d, d ^ mask) for d in range(ways)])
+        full = lax.dynamic_update_slice_in_dim(full, part_2, (here ^ mask) * height, axis=0)
+    every = full
     every = every.reshape((data_devices * mine.shape[0],) + mine.shape[1:])
     return jnp.take(every, block_slot, axis=0)
 

time: 177 us -> 187 us (1.056)
  waiting for transfers between devices: 14.8 us -> 21.5 us
  starting transfers between devices: 16.9 us -> 21.7 us
    ppermute x0 -> x7, starting transfers between devices: none -> 13.1 us  [gather_blocks(): part_2 = lax.ppermute(part_2, 'dp', [(d, d ^ mask) for d in range(ways)])]
    all_to_all x1 -> x0, starting transfers between devices: 7.25 us -> none  [gather_blocks(): lax.all_to_all(jnp.broadcast_to(mine[None], (data_devices,) + mine.shape)...]
    ppermute x0 -> x7, waiting for transfers between devices: none -> 6.71 us  [gather_blocks(): part_2 = lax.ppermute(part_2, 'dp', [(d, d ^ mask) for d in range(ways)])]
  transfers between devices with their start and end apart: 3 -> 9, of which waited for: 2 -> 4; matrix products, arithmetic and copies ran while one was open for 6% -> 6% of each run, Pallas kernels for 0% -> 0%
where the time goes in v1:
time: 187 us; the launch traced here: 186 us
  matrix products  44.7 us (24%)
  local copies, waits for them, and re-layouts  38.8 us (21%)
  blocking collectives  34.4 us (18%)
  starting transfers between devices  21.7 us (12%)
  waiting for transfers between devices  21.5 us (11%)
  other arithmetic  20.9 us (11%)
  between operations  4 us (2%)
    all_to_all x1, waiting for transfers between devices, local(): lax.all_to_all(message, 'head', split_axis=0, concat_axis=0, tiled=True)  14.2 us
    ppermute x7, starting transfers between devices, gather_blocks(): part_2 = lax.ppermute(part_2, 'dp', [(d, d ^ mask) for d in range(ways)])  13.1 us
    unnamed x159, local copies, waits for them, and re-layouts  10.6 us
    all_gather x1, blocking collectives, local(): ffn_blocks = lax.all_gather(blocks[4:12], 'head', axis=0)  9.25 us
    reduce_sum x1, other arithmetic, conv_back(): jnp.sum(grad_grid * shifted(padded_hidden, row_off, col_off), axis=(0, 1,...  7.31 us
    all_gather x1, blocking collectives, local(): attn_blocks = lax.all_gather(blocks[0:4], 'head', axis=0)  6.84 us
    ppermute x7, waiting for transfers between devices, gather_blocks(): part_2 = lax.ppermute(part_2, 'dp', [(d, d ^ mask) for d in range(ways)])  6.71 us
    all_gather x1, blocking collectives, local(): lax.all_gather(my_token_grad.astype(jnp.bfloat16), 'head', axis=0, tiled=...  6.68 us
  transfers between devices with their start and end apart: 9, of which 4 were waited for; matrix products, arithmetic and copies ran while one was open for 6% of the time, Pallas kernels for 0%

profile of v1, /device:TPU:0, one launch (start us, length us, event | category | flops | bytes accessed | tf_op | source)
XLA Modules:
  0.0 185.9 jit_solution(8420810982051407902)
XLA Ops:
  0.7 1.0 convert_bitcast_fusion
  1.7 6.0 %collective-permute-start.6 = (bf16[1,2,54,216]{3,1,2,0:T(2,128)(2,1)S(1)}, bf16[1,2,54,216]{3,1,2,0:T(2,128)(2,1)S(1)}, u32[]{:S(2)}, u32[]{:S(2)}) collective-permute-start(bf16[1,2,54,216]{3,1,2,0:T(2,128)(2,1)S(1)} %convert_bitcast_fusion), channel_id=1, source_target_pairs={{0,28},{4,24},{8,20},{12,16},{16,12},{20,8},{24,4},{28,0},{1,29},{... | collective-permute-start | bytes 139976 | tf_op jit(solution)/shard_map/ppermute | solution.py:116
  7.9 0.8 collective-permute-start.4
  8.7 2.0 %collective-permute-start.3 = (bf16[1,2,54,216]{3,1,2,0:T(2,128)(2,1)S(1)}, bf16[1,2,54,216]{3,1,2,0:T(2,128)(2,1)S(1)}, u32[]{:S(2)}, u32[]{:S(2)}) collective-permute-start(bf16[1,2,54,216]{3,1,2,0:T(2,128)(2,1)S(1)} %convert_bitcast_fusion), channel_id=1, source_target_pairs={{0,16},{4,20},{8,24},{12,28},{16,0},{20,4},{24,8},{28,12},{1,17},{... | collective-permute-start | bytes 139976 | tf_op jit(solution)/shard_map/ppermute | solution.py:116
  10.7 1.6 collective-permute-start
  15.0 0.8 fusion.145
  15.8 5.5 %all-gather.2 = f32[4,216,9]{1,2,0:T(8,128)S(1)} all-gather(f32[1,216,9]{1,2,0:T(8,128)} %bitcast.277), channel_id=1, replica_groups=mesh['dp'=8,'head'=4] {'head'}, dimensions={0}, use_global_device_ids=true | all-gather | bytes 38880 | tf_op jit(solution)/shard_map/all_gather | solution.py:170
  21.5 0.9 constant_dynamic-slice_fusion
  22.4 1.2 constant_dynamic-slice_fusion.1
  25.4 1.2 collective-permute-start.1
  26.7 2.9 %collective-permute-done.1 = bf16[1,2,54,216]{3,1,2,0:T(2,128)(2,1)S(1)} collective-permute-done((bf16[1,2,54,216]{3,1,2,0:T(2,128)(2,1)S(1)}, bf16[1,2,54,216]{3,1,2,0:T(2,128)(2,1)S(1)}, u32[]{:S(2)}, u32[]{:S(2)}) %collective-permute-start.1) | collective-permute-done | bytes 46688 | tf_op jit(solution)/shard_map/ppermute | solution.py:116
  29.6 1.2 collective-permute-start.2
  30.9 3.8 %collective-permute-done.2 = bf16[1,2,54,216]{3,1,2,0:T(2,128)(2,1)S(1)} collective-permute-done((bf16[1,2,54,216]{3,1,2,0:T(2,128)(2,1)S(1)}, bf16[1,2,54,216]{3,1,2,0:T(2,128)(2,1)S(1)}, u32[]{:S(2)}, u32[]{:S(2)}) %collective-permute-start.2) | collective-permute-done | bytes 46688 | tf_op jit(solution)/shard_map/ppermute | solution.py:116
  35.5 6.8 %all-gather = bf16[16,54,216]{2,1,0:T(8,128)(2,1)S(1)} all-gather(bf16[4,54,216]{2,1,0:T(8,128)(2,1)S(1)} %slice.225), channel_id=2, replica_groups=mesh['dp'=8,'head'=4] {'head'}, dimensions={0}, use_global_device_ids=true | all-gather | bytes 466560 | tf_op jit(solution)/shard_map/all_gather | solution.py:168
  45.3 9.3 %all-gather.1 = bf16[32,54,216]{2,0,1:T(8,128)(2,1)S(1)} all-gather(bf16[8,54,216]{2,0,1:T(8,128)(2,1)S(1)} %copy.318), channel_id=3, replica_groups=mesh['dp'=8,'head'=4] {'head'}, dimensions={0}, use_global_device_ids=true | all-gather | bytes 933120 | tf_op jit(solution)/shard_map/all_gather | solution.py:169
  55.0 1.0 reshape.516
  56.9 2.0 %bitcast_reduce_fusion = (f32[12,196]{0,1:T(8,128)S(1)}, f32[196,196,12]{1,2,0:T(8,128)S(1)}) fusion(f32[2,12,12]{2,1,0:T(8,128)S(1)} %copy.313, bf16[12,196,196]{2,1,0:T(8,128)(2,1)S(1)} %multiply_convert_fusion), kind=kOutput, calls=%fused_computation.15 | convolution fusion | flops 66841488 | bytes 3090368 | tf_op jit(solution)/shard_map/mn,gnqk->gmqk/dot_general | solution.py:68
  58.9 1.1 fusion.12
  60.6 3.9 %fusion.28 = bf16[12,196,196]{2,0,1:T(8,128)(2,1)S(1)} fusion(f32[2,12,12]{2,1,0:T(8,128)S(1)} %copy.313, f32[196,196,12]{1,2,0:T(8,128)S(1)} %get-tuple-element.163, f32[12,196]{0,1:T(8,128)S(1)} %fusion.12, f32[12,196]{0,1:T(8,128)S(1)} %get-tuple-element.162), kind=kOutput, calls=%fused_computation.30 | convolution fusion | flops 67765824 | bytes 4346240 | tf_op jit(solution)/shard_map/jm,gmqk->gjqk/dot_general | solution.py:72
  64.6 1.2 copy-done.3
  67.0 1.2 fusion.111
  68.1 1.2 reshape.515
  69.3 1.8 multiply_convert_fusion.1
  71.1 2.1 %reshape.518 = f32[196,864]{1,0:T(8,128)} reshape(f32[1,14,14,864]{3,2,1,0:T(8,128)} %get-tuple-element.144) | data formatting | bytes 1354752 | tf_op jit(solution)/shard_map/reshape | solution.py:48
  73.2 2.0 %fusion.81 = bf16[864,196]{0,1:T(8,128)(2,1)} fusion(f32[864]{0:T(1024)S(1)} %fusion.125, f32[196,864]{1,0:T(8,128)} %reshape.518), kind=kLoop, calls=%fused_computation.123 | loop fusion | flops 1016064 | bytes 1019520 | tf_op jit(solution)/shard_map/gsu,gsd->ud/dot_general | solution.py:218
  75.2 3.5 %multiply_reduce_fusion.8 = (f32[864]{0:T(1024)}, f32[196,864]{1,0:T(8,128)}) fusion(f32[196,864]{1,0:T(8,128)} %fusion.111, f32[196,864]{1,0:T(8,128)} %reshape.518, f32[864]{0:T(1024)S(1)} %fusion.125, bf16[864,216]{1,0:T(8,128)(2,1)} %reshape.516, f32[]{:T(128)} %bitcast.31, f32[1,196,216]{2,0,1:T(1,128)} %constant_dynamic-slice_fusion), kind=kOutput, calls=%fused_computation.116 | convolution fusion | flops 75103200 | bytes 2581636 | tf_op jit(solution)/shard_map/gsd,ud->gsu/dot_general | solution.py:220
  78.7 2.1 %reshape.519 = f32[1,14,14,864]{3,2,1,0:T(8,128)} reshape(f32[196,864]{1,0:T(8,128)} %get-tuple-element.171) | data formatting | bytes 1354752 | tf_op jit(solution)/shard_map/reshape | solution.py:36
  80.8 7.3 %multiply_reduce_fusion = (f32[864]{0:T(1024)}, f32[864]{0:T(1024)}, f32[864]{0:T(1024)}, f32[864]{0:T(1024)}, f32[864]{0:T(1024)}, /*index=5*/f32[864]{0:T(1024...) fusion(f32[1,14,14,864]{3,2,1,0:T(8,128)} %reshape.519, f32[1,14,14,864]{3,2,1,0:T(8,128)S(1)} %reshape.515, ...), kind=kLoop, calls=%fused_computation.106 | loop fusion | flops 5750784 | bytes 1752192 | tf_op jit(solution)/shard_map/reduce_sum | solution.py:62
  88.1 1.2 convert_element_type.227
  89.3 1.8 fusion.97
  91.1 1.4 fusion.136
  92.5 1.1 fusion.100
  93.6 1.1 fusion.36
  94.7 1.9 %fusion.44 = bf16[1,196,12,18]{1,3,2,0:T(8,128)(2,1)S(1)} fusion(bf16[196,12,18]{0,2,1:T(8,128)(2,1)S(1)} %fusion.36, bf16[12,196,196]{2,0,1:T(8,128)(2,1)} %copy-done.3), kind=kOutput, calls=%fused_computation.62 | convolution fusion | flops 16638048 | bytes 1091328 | tf_op jit(solution)/shard_map/ghqk,gqhe->gkhe/dot_general | solution.py:242
  97.2 3.4 %fusion.48 = f32[12,12]{1,0:T(8,128)} fusion(bf16[12,196,196]{2,1,0:T(8,128)(2,1)S(1)} %convolution_convert_fusion, f32[196,196,12]{1,2,0:T(8,128)S(1)} %copy-done.2, f32[12,196]{0,1:T(8,128)S(1)} %copy-done.27, f32[12,196]{0,1:T(8,128)S(1)} %copy-done.23), kind=kOutput, calls=%fused_computation.66 | convolution fusion | flops 67304832 | bytes 2785344 | tf_op jit(solution)/shard_map/gjqk,gmqk->jm/dot_general | solution.py:80
  100.6 4.1 %fusion.4 = (f32[12,196]{0,1:T(8,128)S(1)}, f32[196,196,12]{1,2,0:T(8,128)S(1)}) fusion(f32[12,196]{0,1:T(8,128)S(1)} %copy-done.27, f32[12,196]{0,1:T(8,128)S(1)} %copy-done.23, f32[196,196,12]{1,2,0:T(8,128)S(1)} %copy-done.2, f32[2,12,12]{2,1,0:T(8,128)S(1)} %copy.313, bf16[12,196,196]{2,1,0:T(8,128)(2,1)S(1)} %convolution_convert_fusion), kind=kOutput, calls=%fused_computation.8 | convolution fusion | flops 68224464 | bytes 6506432 | tf_op jit(solution)/shard_map/jm,gjqk->gmqk/dot_general | solution.py:79
  104.7 3.8 %fusion.53 = f32[12,12]{1,0:T(8,128)} fusion(bf16[12,196,196]{2,1,0:T(8,128)(2,1)S(1)} %multiply_convert_fusion, f32[12,196]{0,1:T(8,128)S(1)} %get-tuple-element.167, f32[196,196,12]{1,2,0:T(8,128)S(1)} %get-tuple-element.168, f32[196,196,12]{1,2,0:T(8,128)S(1)} %copy-done.2, f32[12,196]{0,1:T(8,128)S(1)} %copy-done.27, f32[12,196]{0,1:T(8,128)S(1)} %copy-done.23), kind=kOutput, calls=%fused_computation.67 | convolution fusion | flops 68226816 | bytes 4638720 | tf_op jit(solution)/shard_map/gmqk,gnqk->mn/dot_general | solution.py:82
  108.5 4.7 %fusion.25 = bf16[12,196,196]{2,0,1:T(8,128)(2,1)S(1)} fusion(f32[196,196,12]{1,2,0:T(8,128)S(1)} %get-tuple-element.168, f32[12,196]{0,1:T(8,128)S(1)} %get-tuple-element.167, f32[2,12,12]{2,1,0:T(8,128)S(1)} %copy.313, f32[196,196,12]{1,2,0:T(8,128)S(1)} %copy-done.2, f32[12,196]{0,1:T(8,128)S(1)} %copy-done.27, f32[12,196]{0,1:T(8,128)S(1)} %copy-done.23), kind=kOutput, calls=%fused_computation.29 | convolution fusion | flops 68687808 | bytes 7659904 | tf_op jit(solution)/shard_map/mn,gmqk->gnqk/dot_general | solution.py:85
  113.4 1.1 fusion.45
  114.6 1.1 fusion.46
  117.3 0.8 convolution_convert_fusion.4
  119.0 1.1 copy.336
  120.2 1.0 convolution_convert_fusion.5
  121.1 0.8 copy.335
  122.2 1.0 reshape.524
  123.2 1.1 fusion.147
  124.3 1.1 convolution_add_fusion.1
  125.4 1.2 fusion.95
  126.8 1.0 convolution_convert_fusion.7
  128.3 0.8 copy.334
  129.3 0.9 copy.338
  130.2 0.9 copy.337
  131.1 3.8 %concatenate.19 = bf16[4,678,216]{1,2,0:T(8,128)(2,1)} concatenate(bf16[4,54,216]{1,2,0:T(8,128)(2,1)S(1)} %copy.333, bf16[4,54,216]{1,2,0:T(8,128)(2,1)} %copy.334, bf16[4,54,216]{1,2,0:T(8,128)(2,1)} %copy.335, bf16[4,54,216]{1,2,0:T(8,128)(2,1)S(1)} %copy.336, bf16[4,216,216]{1,2,0:T(8,128)(2,1)S(1)} %convolution_convert_fusion.2, ...), dimensions={1} | concatenate | bytes 2343168 | tf_op jit(solution)/shard_map/concatenate | solution.py:297
  134.9 3.5 %all-to-all-start = ((bf16[4,678,216]{1,2,0:T(8,128)(2,1)}), bf16[4,678,216]{1,2,0:T(8,128)(2,1)S(1)}, u32[]{:S(2)}, u32[]{:S(2)}) async-start(bf16[4,678,216]{1,2,0:T(8,128)(2,1)} %concatenate.19), calls=%async_computation | async-start | bytes 2654208 | tf_op jit(solution)/shard_map/all_to_all | solution.py:302
  138.4 1.9 %convert_element_type.222 = bf16[196,864]{1,0:T(8,128)(2,1)} reshape(bf16[1,14,14,864]{3,2,1,0:T(8,128)(2,1)} %get-tuple-element.143) | data formatting | bytes 677376 | tf_op jit(solution)/shard_map/convert_element_type | solution.py:210
  140.3 1.3 fusion.43
  141.6 14.2 %all-to-all-done = bf16[4,678,216]{1,2,0:T(8,128)(2,1)S(1)} async-done(((bf16[4,678,216]{1,2,0:T(8,128)(2,1)}), bf16[4,678,216]{1,2,0:T(8,128)(2,1)S(1)}, u32[]{:S(2)}, u32[]{:S(2)}) %all-to-all-start) | async-done | bytes 1171616 | tf_op jit(solution)/shard_map/all_to_all | solution.py:302
  156.7 1.1 scatter_fusion
  158.0 0.9 pad_maximum_fusion
  159.0 5.0 %all-to-all-start.1 = ((bf16[8,138,216]{2,1,0:T(8,128)(2,1)}), bf16[8,138,216]{2,1,0:T(8,128)(2,1)S(1)}, u32[]{:S(2)}, u32[]{:S(2)}) async-start(bf16[8,138,216]{2,1,0:T(8,128)(2,1)} %pad_maximum_fusion), calls=%async_computation.1 | async-start | bytes 1179648 | tf_op jit(solution)/shard_map/all_to_all | solution.py:320
  164.0 6.2 %all_gather.26 = bf16[4,196,216]{2,1,0:T(8,128)(2,1)S(1)} all-gather(bf16[1,196,216]{2,1,0:T(8,128)(2,1)S(1)} %fusion.43), channel_id=1, replica_groups=mesh['dp'=8,'head'=4] {'head'}, dimensions={0}, use_global_device_ids=true | all-gather | bytes 423360 | tf_op jit(solution)/shard_map/all_gather | solution.py:213
  170.2 1.0 copy.349
  171.4 6.7 %all_gather.27 = bf16[4,196,216]{2,1,0:T(8,128)(2,1)S(1)} all-gather(bf16[1,196,216]{2,1,0:T(8,128)(2,1)S(1)} %fusion.94), channel_id=1, replica_groups=mesh['dp'=8,'head'=4] {'head'}, dimensions={0}, use_global_device_ids=true | all-gather | bytes 423360 | tf_op jit(solution)/shard_map/all_gather | solution.py:275
  178.1 1.0 copy.350
  (265 shorter events, 21.4 us)
Async XLA Ops:
  0.6 20.9 %copy-start = (f32[4,196,216]{2,0,1:T(4,128)S(1)}, f32[4,196,216]{2,0,1:T(4,128)}, u32[]{:S(2)}) copy-start(f32[4,196,216]{2,0,1:T(4,128)} %param.19) | copy-start | bytes 2032132
  1.7 33.1 %collective-permute-start.6 = (bf16[1,2,54,216]{3,1,2,0:T(2,128)(2,1)S(1)}, bf16[1,2,54,216]{3,1,2,0:T(2,128)(2,1)S(1)}, u32[]{:S(2)}, u32[]{:S(2)}) collective-permute-start(bf16[1,2,54,216]{3,1,2,0:T(2,128)(2,1)S(1)} %convert_bitcast_fusion), channel_id=1, source_target_pairs={{0,28},{4,24},{8,20},{12,16},{16,12},{20,8},{24,4},{28,0},{1,29},{... | collective-permute-start | bytes 139976 | tf_op jit(solution)/shard_map/ppermute | solution.py:116
  7.7 27.0 %collective-permute-start.5 = (bf16[1,2,54,216]{3,1,2,0:T(2,128)(2,1)S(1)}, bf16[1,2,54,216]{3,1,2,0:T(2,128)(2,1)S(1)}, u32[]{:S(2)}, u32[]{:S(2)}) collective-permute-start(bf16[1,2,54,216]{3,1,2,0:T(2,128)(2,1)S(1)} %convert_bitcast_fusion), channel_id=1, source_target_pairs={{0,24},{4,28},{8,16},{12,20},{16,8},{20,12},{24,0},{28,4},{1,25},{... | collective-permute-start | bytes 139976 | tf_op jit(solution)/shard_map/ppermute | solution.py:116
  7.9 26.8 %collective-permute-start.4 = (bf16[1,2,54,216]{3,1,2,0:T(2,128)(2,1)S(1)}, bf16[1,2,54,216]{3,1,2,0:T(2,128)(2,1)S(1)}, u32[]{:S(2)}, u32[]{:S(2)}) collective-permute-start(bf16[1,2,54,216]{3,1,2,0:T(2,128)(2,1)S(1)} %convert_bitcast_fusion), channel_id=1, source_target_pairs={{0,20},{4,16},{8,28},{12,24},{16,4},{20,0},{24,12},{28,8},{1,21},{... | collective-permute-start | bytes 139976 | tf_op jit(solution)/shard_map/ppermute | solution.py:116
  8.7 26.0 %collective-permute-start.3 = (bf16[1,2,54,216]{3,1,2,0:T(2,128)(2,1)S(1)}, bf16[1,2,54,216]{3,1,2,0:T(2,128)(2,1)S(1)}, u32[]{:S(2)}, u32[]{:S(2)}) collective-permute-start(bf16[1,2,54,216]{3,1,2,0:T(2,128)(2,1)S(1)} %convert_bitcast_fusion), channel_id=1, source_target_pairs={{0,16},{4,20},{8,24},{12,28},{16,0},{20,4},{24,8},{28,12},{1,17},{... | collective-permute-start | bytes 139976 | tf_op jit(solution)/shard_map/ppermute | solution.py:116
  10.7 14.7 %collective-permute-start = (bf16[1,2,54,216]{3,1,2,0:T(2,128)(2,1)S(1)}, bf16[1,2,54,216]{3,1,2,0:T(2,128)(2,1)S(1)}, u32[]{:S(2)}, u32[]{:S(2)}) collective-permute-start(bf16[1,2,54,216]{3,1,2,0:T(2,128)(2,1)S(1)} %convert_bitcast_fusion), channel_id=1, source_target_pairs={{0,4},{4,0},{8,12},{12,8},{16,20},{20,16},{24,28},{28,24},{1,5},{5... | collective-permute-start | bytes 139976 | tf_op jit(solution)/shard_map/ppermute | solution.py:116
  13.0 9.4 %copy-start.64 = (s32[12]{0:T(128)}, s32[12]{0:T(128)S(1)}, u32[]{:S(2)}) copy-start(s32[12]{0:T(128)S(1)} %compare_select_fusion) | copy-start | bytes 148
  15.8 28.4 %copy-start.38 = (f32[1,216]{1,0:T(1,128)}, f32[1,216]{1,0:T(1,128)S(1)}, u32[]{:S(2)}) copy-start(f32[1,216]{1,0:T(1,128)S(1)} %get-tuple-element.160) | copy-start | bytes 2596
  15.8 28.4 %copy-start.67 = (f32[1,216]{1,0:T(1,128)}, f32[1,216]{1,0:T(1,128)S(1)}, u32[]{:S(2)}) copy-start(f32[1,216]{1,0:T(1,128)S(1)} %get-tuple-element.159) | copy-start | bytes 2596
  15.8 51.0 %copy-start.32 = (f32[1,216]{1,0:T(1,128)}, f32[1,216]{1,0:T(1,128)S(1)}, u32[]{:S(2)}) copy-start(f32[1,216]{1,0:T(1,128)S(1)} %get-tuple-element.158) | copy-start | bytes 2596
  15.8 51.0 %copy-start.55 = (f32[1,216]{1,0:T(1,128)}, f32[1,216]{1,0:T(1,128)S(1)}, u32[]{:S(2)}) copy-start(f32[1,216]{1,0:T(1,128)S(1)} %get-tuple-element.161) | copy-start | bytes 2596
  23.7 42.6 %copy-start.4 = (bf16[1,196,216]{2,1,0:T(8,128)(2,1)}, bf16[1,196,216]{2,1,0:T(8,128)(2,1)S(1)}, u32[]{:S(2)}) copy-start(bf16[1,196,216]{2,1,0:T(8,128)(2,1)S(1)} %get-tuple-element.146) | copy-start | bytes 254020
  23.7 20.5 %copy-start.36 = (f32[196]{0:T(256)}, f32[196]{0:T(256)S(1)}, u32[]{:S(2)}) copy-start(f32[196]{0:T(256)S(1)} %broadcast_multiply_fusion.5) | copy-start | bytes 2356
  24.0 20.3 %copy-start.53 = (f32[196]{0:T(256)}, f32[196]{0:T(256)S(1)}, u32[]{:S(2)}) copy-start(f32[196]{0:T(256)S(1)} %add_rsqrt_fusion.1) | copy-start | bytes 2356
  24.0 40.5 %copy-start.66 = (f32[12]{0:T(128)}, f32[12]{0:T(128)S(1)}, u32[]{:S(2)}) copy-start(f32[12]{0:T(128)S(1)} %compare_convert_fusion) | copy-start | bytes 148
  25.4 4.2 %collective-permute-start.1 = (bf16[1,2,54,216]{3,1,2,0:T(2,128)(2,1)S(1)}, bf16[1,2,54,216]{3,1,2,0:T(2,128)(2,1)S(1)}, u32[]{:S(2)}, u32[]{:S(2)}) collective-permute-start(bf16[1,2,54,216]{3,1,2,0:T(2,128)(2,1)S(1)} %convert_bitcast_fusion), channel_id=1, source_target_pairs={{0,8},{4,12},{8,0},{12,4},{16,24},{20,28},{24,16},{28,20},{1,9},{5... | collective-permute-start | bytes 139976 | tf_op jit(solution)/shard_map/ppermute | solution.py:116
  29.6 5.1 %collective-permute-start.2 = (bf16[1,2,54,216]{3,1,2,0:T(2,128)(2,1)S(1)}, bf16[1,2,54,216]{3,1,2,0:T(2,128)(2,1)S(1)}, u32[]{:S(2)}, u32[]{:S(2)}) collective-permute-start(bf16[1,2,54,216]{3,1,2,0:T(2,128)(2,1)S(1)} %convert_bitcast_fusion), channel_id=1, source_target_pairs={{0,12},{4,8},{8,4},{12,0},{16,28},{20,24},{24,20},{28,16},{1,13},{... | collective-permute-start | bytes 139976 | tf_op jit(solution)/shard_map/ppermute | solution.py:116
  43.2 11.6 %copy-start.18 = (bf16[216,216]{1,0:T(8,128)(2,1)}, bf16[216,216]{1,0:T(8,128)(2,1)S(1)}, u32[]{:S(2)}) copy-start(bf16[216,216]{1,0:T(8,128)(2,1)S(1)} %reshape_squeeze.14) | copy-start | bytes 279940
  43.7 12.7 %copy-start.9 = (bf16[196,12,18]{0,2,1:T(8,128)(2,1)}, bf16[196,12,18]{0,2,1:T(8,128)(2,1)S(1)}, u32[]{:S(2)}) copy-start(bf16[196,12,18]{0,2,1:T(8,128)(2,1)S(1)} %reshape.509) | copy-start | bytes 254020
  43.7 11.1 %copy-start.20 = (bf16[216,216]{1,0:T(8,128)(2,1)}, bf16[216,216]{1,0:T(8,128)(2,1)S(1)}, u32[]{:S(2)}) copy-start(bf16[216,216]{1,0:T(8,128)(2,1)S(1)} %reshape_squeeze.13) | copy-start | bytes 279940
  44.1 12.2 %copy-start.11 = (bf16[196,12,18]{0,2,1:T(8,128)(2,1)}, bf16[196,12,18]{0,2,1:T(8,128)(2,1)S(1)}, u32[]{:S(2)}) copy-start(bf16[196,12,18]{0,2,1:T(8,128)(2,1)S(1)} %reshape.508) | copy-start | bytes 254020
  45.3 19.3 %copy-start.13 = (bf16[196,12,18]{0,2,1:T(8,128)(2,1)}, bf16[196,12,18]{0,2,1:T(8,128)(2,1)S(1)}, u32[]{:S(2)}) copy-start(bf16[196,12,18]{0,2,1:T(8,128)(2,1)S(1)} %reshape.507) | copy-start | bytes 254020
  58.8 5.7 %copy-start.1 = (f32[196,196,12]{1,2,0:T(8,128)}, f32[196,196,12]{1,2,0:T(8,128)S(1)}, u32[]{:S(2)}) copy-start(f32[196,196,12]{1,2,0:T(8,128)S(1)} %get-tuple-element.163) | copy-start | bytes 5531908
  58.9 5.7 %copy-start.22 = (f32[12,196]{0,1:T(8,128)}, f32[12,196]{0,1:T(8,128)S(1)}, u32[]{:S(2)}) copy-start(f32[12,196]{0,1:T(8,128)S(1)} %get-tuple-element.162) | copy-start | bytes 28228
  66.6 6.5 %copy-start.30 = (f32[196]{0:T(256)}, f32[196]{0:T(256)S(1)}, u32[]{:S(2)}) copy-start(f32[196]{0:T(256)S(1)} %broadcast_multiply_fusion.4) | copy-start | bytes 2356
  66.9 6.3 %copy-start.34 = (f32[196]{0:T(256)}, f32[196]{0:T(256)S(1)}, u32[]{:S(2)}) copy-start(f32[196]{0:T(256)S(1)} %add_rsqrt_fusion) | copy-start | bytes 2356
  88.1 8.5 %copy-start.14 = (bf16[196,12,18]{0,2,1:T(8,128)(2,1)S(1)}, bf16[196,12,18]{0,2,1:T(8,128)(2,1)}, u32[]{:S(2)}) copy-start(bf16[196,12,18]{0,2,1:T(8,128)(2,1)} %copy-done.13) | copy-start | bytes 254020
  88.1 9.1 %copy-start.23 = (f32[12,196]{0,1:T(8,128)S(1)}, f32[12,196]{0,1:T(8,128)}, u32[]{:S(2)}) copy-start(f32[12,196]{0,1:T(8,128)} %copy-done.22) | copy-start | bytes 28228
  88.1 9.1 %copy-start.27 = (f32[12,196]{0,1:T(8,128)S(1)}, f32[12,196]{0,1:T(8,128)}, u32[]{:S(2)}) copy-start(f32[12,196]{0,1:T(8,128)} %copy-done.26) | copy-start | bytes 28228
  89.3 7.9 %copy-start.2 = (f32[196,196,12]{1,2,0:T(8,128)S(1)}, f32[196,196,12]{1,2,0:T(8,128)}, u32[]{:S(2)}) copy-start(f32[196,196,12]{1,2,0:T(8,128)} %copy-done.1) | copy-start | bytes 5531908
  108.5 4.7 %copy-start.12 = (bf16[196,12,18]{0,2,1:T(8,128)(2,1)S(1)}, bf16[196,12,18]{0,2,1:T(8,128)(2,1)}, u32[]{:S(2)}) copy-start(bf16[196,12,18]{0,2,1:T(8,128)(2,1)} %copy-done.11) | copy-start | bytes 254020
  108.5 6.1 %copy-start.10 = (bf16[196,12,18]{0,2,1:T(8,128)(2,1)S(1)}, bf16[196,12,18]{0,2,1:T(8,128)(2,1)}, u32[]{:S(2)}) copy-start(bf16[196,12,18]{0,2,1:T(8,128)(2,1)} %copy-done.9) | copy-start | bytes 254020
  108.5 7.2 %copy-start.16 = (bf16[196,216]{0,1:T(8,128)(2,1)S(1)}, bf16[196,216]{0,1:T(8,128)(2,1)}, u32[]{:S(2)}) copy-start(bf16[196,216]{0,1:T(8,128)(2,1)} %copy-done.15) | copy-start | bytes 254020
  113.4 3.8 %copy-start.40 = (f32[864]{0:T(1024)S(1)}, f32[864]{0:T(1024)}, u32[]{:S(2)}) copy-start(f32[864]{0:T(1024)} %get-tuple-element.112) | copy-start | bytes 10372
  113.4 5.1 %copy-start.31 = (f32[196]{0:T(256)S(1)}, f32[196]{0:T(256)}, u32[]{:S(2)}) copy-start(f32[196]{0:T(256)} %copy-done.30) | copy-start | bytes 2356
  113.4 5.1 %copy-start.33 = (f32[1,216]{1,0:T(1,128)S(1)}, f32[1,216]{1,0:T(1,128)}, u32[]{:S(2)}) copy-start(f32[1,216]{1,0:T(1,128)} %copy-done.32) | copy-start | bytes 2596
  113.4 5.1 %copy-start.35 = (f32[196]{0:T(256)S(1)}, f32[196]{0:T(256)}, u32[]{:S(2)}) copy-start(f32[196]{0:T(256)} %copy-done.34) | copy-start | bytes 2356
  113.4 5.1 %copy-start.56 = (f32[1,216]{1,0:T(1,128)S(1)}, f32[1,216]{1,0:T(1,128)}, u32[]{:S(2)}) copy-start(f32[1,216]{1,0:T(1,128)} %copy-done.55) | copy-start | bytes 2596
  114.6 5.5 %copy-start.5 = (bf16[1,196,216]{2,1,0:T(8,128)(2,1)S(1)}, bf16[1,196,216]{2,1,0:T(8,128)(2,1)}, u32[]{:S(2)}) copy-start(bf16[1,196,216]{2,1,0:T(8,128)(2,1)} %copy-done.4) | copy-start | bytes 254020
  114.6 5.5 %copy-start.37 = (f32[196]{0:T(256)S(1)}, f32[196]{0:T(256)}, u32[]{:S(2)}) copy-start(f32[196]{0:T(256)} %copy-done.36) | copy-start | bytes 2356
  114.6 5.6 %copy-start.39 = (f32[1,216]{1,0:T(1,128)S(1)}, f32[1,216]{1,0:T(1,128)}, u32[]{:S(2)}) copy-start(f32[1,216]{1,0:T(1,128)} %copy-done.38) | copy-start | bytes 2596
  114.6 5.6 %copy-start.54 = (f32[196]{0:T(256)S(1)}, f32[196]{0:T(256)}, u32[]{:S(2)}) copy-start(f32[196]{0:T(256)} %copy-done.53) | copy-start | bytes 2356
  115.7 6.3 %copy-start.57 = (f32[12,12]{1,0:T(8,128)S(1)}, f32[12,12]{1,0:T(8,128)}, u32[]{:S(2)}) copy-start(f32[12,12]{1,0:T(8,128)} %fusion.48) | copy-start | bytes 1732
  115.7 6.3 %copy-start.58 = (f32[12,12]{1,0:T(8,128)S(1)}, f32[12,12]{1,0:T(8,128)}, u32[]{:S(2)}) copy-start(f32[12,12]{1,0:T(8,128)} %fusion.53) | copy-start | bytes 1732
  116.6 5.6 %copy-start.17 = (bf16[1,196,12,18]{1,3,2,0:T(8,128)(2,1)S(1)}, bf16[1,196,12,18]{1,3,2,0:T(8,128)(2,1)}, u32[]{:S(2)}) copy-start(bf16[1,196,12,18]{1,3,2,0:T(8,128)(2,1)} %fusion.46) | copy-start | bytes 254020
  119.0 9.1 %copy-start.68 = (f32[1,216]{1,0:T(1,128)S(1)}, f32[1,216]{1,0:T(1,128)}, u32[]{:S(2)}) copy-start(f32[1,216]{1,0:T(1,128)} %copy-done.67) | copy-start | bytes 2596
  119.0 10.3 %copy-start.59 = (f32[216]{0:T(256)S(1)}, f32[216]{0:T(256)}, u32[]{:S(2)}) copy-start(f32[216]{0:T(256)} %get-tuple-element.117) | copy-start | bytes 2596
  119.0 10.3 %copy-start.63 = (f32[216]{0:T(256)S(1)}, f32[216]{0:T(256)}, u32[]{:S(2)}) copy-start(f32[216]{0:T(256)} %get-tuple-element.113) | copy-start | bytes 2596
  131.1 9.2 %copy-start.7 = (bf16[864,216]{1,0:T(8,128)(2,1)S(1)}, bf16[864,216]{1,0:T(8,128)(2,1)}, u32[]{:S(2)}) copy-start(bf16[864,216]{1,0:T(8,128)(2,1)} %reshape.516) | copy-start | bytes 1119748
  134.9 21.0 %all-to-all-start = ((bf16[4,678,216]{1,2,0:T(8,128)(2,1)}), bf16[4,678,216]{1,2,0:T(8,128)(2,1)S(1)}, u32[]{:S(2)}, u32[]{:S(2)}) async-start(bf16[4,678,216]{1,2,0:T(8,128)(2,1)} %concatenate.19), calls=%async_computation | async-start | bytes 2654208 | tf_op jit(solution)/shard_map/all_to_all | solution.py:302
  138.4 18.2 %copy-start.65 = (s32[12]{0:T(128)S(1)}, s32[12]{0:T(128)}, u32[]{:S(2)}) copy-start(s32[12]{0:T(128)} %copy-done.64) | copy-start | bytes 148
  158.9 21.0 %copy-start.29 = (f32[2,12,12]{2,0,1:T(2,128)S(1)}, f32[2,12,12]{2,0,1:T(2,128)}, u32[]{:S(2)}) copy-start(f32[2,12,12]{2,0,1:T(2,128)} %param.30) | copy-start | bytes 3460
  158.9 21.0 %copy-start.51 = (f32[2,12,12]{2,0,1:T(2,128)S(1)}, f32[2,12,12]{2,0,1:T(2,128)}, u32[]{:S(2)}) copy-start(f32[2,12,12]{2,0,1:T(2,128)} %param.31) | copy-start | bytes 3460
  158.9 21.0 %copy-start.52 = (f32[2,12,12]{2,0,1:T(2,128)S(1)}, f32[2,12,12]{2,0,1:T(2,128)}, u32[]{:S(2)}) copy-start(f32[2,12,12]{2,0,1:T(2,128)} %param.32) | copy-start | bytes 3460
  158.9 22.9 %copy-start.19 = (f32[2,54,216]{2,0,1:T(2,128)S(1)}, f32[2,54,216]{2,0,1:T(2,128)}, u32[]{:S(2)}) copy-start(f32[2,54,216]{2,0,1:T(2,128)} %param.24) | copy-start | bytes 279940
  158.9 22.9 %copy-start.24 = (f32[2,54,216]{2,0,1:T(2,128)S(1)}, f32[2,54,216]{2,0,1:T(2,128)}, u32[]{:S(2)}) copy-start(f32[2,54,216]{2,0,1:T(2,128)} %param.25) | copy-start | bytes 279940
  158.9 22.9 %copy-start.25 = (f32[2,54,216]{2,0,1:T(2,128)S(1)}, f32[2,54,216]{2,0,1:T(2,128)}, u32[]{:S(2)}) copy-start(f32[2,54,216]{2,0,1:T(2,128)} %param.26) | copy-start | bytes 279940
  159.0 20.7 %all-to-all-start.1 = ((bf16[8,138,216]{2,1,0:T(8,128)(2,1)}), bf16[8,138,216]{2,1,0:T(8,128)(2,1)S(1)}, u32[]{:S(2)}, u32[]{:S(2)}) async-start(bf16[8,138,216]{2,1,0:T(8,128)(2,1)} %pad_maximum_fusion), calls=%async_computation.1 | async-start | bytes 1179648 | tf_op jit(solution)/shard_map/all_to_all | solution.py:320
  170.1 14.5 %copy-start.50 = (f32[4,216]{1,0:T(4,128)S(1)}, f32[4,216]{1,0:T(4,128)}, u32[]{:S(2)}) copy-start(f32[4,216]{1,0:T(4,128)} %param.27) | copy-start | bytes 10372
  170.1 14.5 %copy-start.60 = (f32[4,216]{1,0:T(4,128)S(1)}, f32[4,216]{1,0:T(4,128)}, u32[]{:S(2)}) copy-start(f32[4,216]{1,0:T(4,128)} %param.28) | copy-start | bytes 10372
  170.1 14.5 %copy-start.61 = (f32[4,216]{1,0:T(4,128)S(1)}, f32[4,216]{1,0:T(4,128)}, u32[]{:S(2)}) copy-start(f32[4,216]{1,0:T(4,128)} %param.29) | copy-start | bytes 10372
  170.1 15.1 %copy-start.28 = (f32[9,216]{1,0:T(8,128)S(1)}, f32[9,216]{1,0:T(8,128)}, u32[]{:S(2)}) copy-start(f32[9,216]{1,0:T(8,128)} %param.33) | copy-start | bytes 23332
  170.2 15.1 %copy-start.48 = (f32[9,216]{1,0:T(8,128)S(1)}, f32[9,216]{1,0:T(8,128)}, u32[]{:S(2)}) copy-start(f32[9,216]{1,0:T(8,128)} %param.34) | copy-start | bytes 23332
  170.2 15.1 %copy-start.49 = (f32[9,216]{1,0:T(8,128)S(1)}, f32[9,216]{1,0:T(8,128)}, u32[]{:S(2)}) copy-start(f32[9,216]{1,0:T(8,128)} %param.35) | copy-start | bytes 23332
  (14 other events, 35.7 us)
